TPU v7x, 128 devices: a whole 4x4x4 slice. The times are simulated.
128 devices in a mesh: group: 8 (over y, core), member: 16 (over z, x).
Axes of the slice: x: 4, y: 4, z: 4, core: 2. Of those that a mesh axis runs over, the one named last changes fastest.
Arguments:
- queries: bfloat16 [512, 32, 128], P('group'), may hold values from -0.5 to 0.5
- centroids: bfloat16 [131072, 128], P('member'), may hold values from -0.5 to 0.5
- doc_resid: bfloat16 [32768, 128, 128], P(('group', 'member')), may hold values from -6 to 6
- doc_codes: int32 [32768, 128], P(('group', 'member')), may hold values from 0 to 131071
- doc_scale: bfloat16 [32768], P(('group', 'member')), may hold values from 0.019897461 to 0.19921875
- doc_len: int32 [32768], P(('group', 'member')), may hold values from 1 to 128
- send_list: int32 [128, 128, 2], P(('group', 'member')), may hold values from 0 to 255
- cand: int32 [512, 2048], P('group', 'member'), may hold values from 0 to 255
Outputs:
- scores: float32 [512, 2048], P('group', 'member')
Inputs may be any that keep to these rules, and one draw needn't show every extreme that they name: `cand`: slot s names the document source s div 2 sent to this candidate's device in its slot s mod 2.
All inputs are finite; a program needn't handle non-finite values.
Results may differ from a plain program's by a relative error of at most 0.0003.
Values may be sent and summed in bfloat16 or wider, within the bound.
No kernel may reach another device: no remote copies, remote signals or barrier semaphores. Data moves between devices by JAX's collectives and lax.ppermute only.
A program may use at most 256 MiB of HBM per device.

v0:
```python
import jax
import jax.numpy as jnp
from jax import lax
from jax.sharding import PartitionSpec as P

masked_value = -1000000000.0


def decompress(centroids, codes, residual, scales):
    table = lax.all_gather(centroids, "member", axis=0, tiled=True)
    base = jnp.take(table, codes.reshape(-1), axis=0).astype(jnp.float32)
    base = base.reshape(residual.shape)
    spread = scales.astype(jnp.float32)[:, None, None] * residual.astype(jnp.float32)
    return (base + spread).astype(jnp.bfloat16)


def maxsim(query_block, embedded, lengths):
    count, qtokens, width = query_block.shape
    slots, block = (embedded.shape[0], embedded.shape[1])
    sims = jnp.einsum(
        "rd,cd->rc",
        query_block.reshape(count * qtokens, width),
        embedded.reshape(slots * block, width),
        preferred_element_type=jnp.float32,
    )
    sims = sims.reshape(count, qtokens, slots, block)
    valid = jnp.arange(block, dtype=jnp.int32)[None, :] < lengths[:, None]
    sims = jnp.where(valid[None, None], sims, masked_value)
    return jnp.mean(jnp.max(sims, axis=3), axis=1)


def body(queries, centroids, doc_resid, doc_codes, doc_scale, doc_len, send_list, cand):
    groups = lax.axis_size("group")
    members = lax.axis_size("member")
    capacity = send_list.shape[2]
    held, block, width = (doc_resid.shape[0], doc_resid.shape[1], doc_resid.shape[2])
    per_group = members * capacity
    chosen = send_list[0].reshape(-1)
    residual = jnp.take(doc_resid.reshape(held, block * width), chosen, axis=0).reshape(
        -1, block, width
    )
    codes = jnp.take(doc_codes, chosen, axis=0)
    scales = jnp.take(doc_scale, chosen, axis=0)
    lengths = jnp.take(doc_len, chosen, axis=0)
    qcount, qtokens = (queries.shape[0], queries.shape[1])
    embedded = decompress(centroids, codes, residual, scales)
    every_query = lax.all_gather(queries, "group", axis=0, tiled=True)

    def score_group(items):
        return maxsim(items[0], items[1], items[2])

    local = lax.map(
        score_group,
        (
            every_query.reshape(groups, qcount, qtokens, width),
            embedded.reshape(groups, per_group, block, width),
            lengths.reshape(groups, per_group),
        ),
    )
    local = (
        local.reshape(groups, qcount, members, capacity)
        .transpose(0, 2, 1, 3)
        .reshape(groups * members, qcount, capacity)
    )
    returned = lax.all_to_all(local, ("group", "member"), split_axis=0, concat_axis=0, tiled=True)
    dense = jnp.transpose(returned, (1, 0, 2)).reshape(qcount, -1)
    return jnp.take_along_axis(dense, cand, axis=1)


def solution(mesh):
    placed = (
        P("group", None, None),
        P("member", None),
        P(("group", "member"), None, None),
        P(("group", "member"), None),
        P(("group", "member")),
        P(("group", "member")),
        P(("group", "member"), None, None),
        P("group", "member"),
    )
    return jax.shard_map(
        body, mesh=mesh, in_specs=placed, out_specs=P("group", "member"), check_vma=False
    )
```

profile of v0, /device:TPU:1, one launch (start us, length us, event | category | flops | bytes accessed | tf_op | source)
XLA Modules:
  0.0 885.1 jit_solution(12478388455540469417)
XLA Ops:
  6.5 0.7 all-gather.5.cloned.1.call-update
  7.3 0.7 all-gather.3.cloned.1.call-update
  8.0 0.8 copy.23
  8.8 0.1 reshape_squeeze.8
  8.9 0.1 reshape_squeeze.7
  9.0 0.1 reshape_squeeze.9
  9.2 1.9 gather_fusion.3
  11.1 0.1 gather.41
  11.2 0.7 gather_fusion.1
  12.0 23.1 %copy.36 = bf16[32,8,128,128]{3,1,2,0:T(8,128)(2,1)} copy(bf16[32,8,128,128]{3,2,1,0:T(8,128)(2,1)} %bitcast.63) | data formatting | bytes 16777216
  35.1 21.2 %gather_fusion.4 = bf16[256,16384]{1,0:T(8,128)(2,1)} fusion(bf16[256,16384]{1,0:T(8,128)(2,1)} %bitcast.59, s32[1024]{0:T(1024)S(1)} %pad_clamp_fusion), kind=kCustom, calls=%fused_computation.4 | custom fusion | bytes 16778240 | tf_op jit(solution)/shard_map/jit(_take)/gather | solution.py:39
  56.2 9.2 %copy.33 = bf16[32,8,128,128]{3,2,1,0:T(8,128)(2,1)} copy(bf16[32,8,128,128]{3,1,2,0:T(8,128)(2,1)} %bitcast.61) | data formatting | bytes 16777216
  65.4 2.2 gather_fusion
  67.7 0.1 broadcast_select_fusion
  67.8 0.1 compare_and_fusion
  67.9 0.1 compare_select_fusion
  68.1 141.8 %all-gather.5.cloned.1.call-done = bf16[131072,128]{1,0:T(8,128)(2,1)} async-done(((bf16[8192,128]{1,0:T(8,128)(2,1)}), bf16[131072,128]{1,0:T(8,128)(2,1)}) %all-gather.5.cloned.1.call-update) | async-done | bytes 33554448 | tf_op jit(solution)/shard_map/all_gather | solution.py:10
  210.0 492.6 %gather_fusion.2 = bf16[32768,128]{1,0:T(8,128)(2,1)} fusion(bf16[131072,128]{1,0:T(8,128)(2,1)} %all-gather.5.cloned.1.call-done, s32[32768]{0:T(1024)S(1)} %broadcast_clamp_fusion), kind=kCustom, calls=%fused_computation.2 | custom fusion | bytes 16908288 | tf_op jit(solution)/shard_map/jit(_take)/gather | solution.py:11
  702.6 9.5 %add_convert_fusion = bf16[8,32,128,128]{3,2,1,0:T(8,128)(2,1)} fusion(f32[8,32]{1,0:T(8,128)S(1)} %get-tuple-element.43, bf16[8,32,128,128]{3,2,1,0:T(8,128)(2,1)} %bitcast.60, pred[8,32]{1,0:T(8,128)(4,1)S(1)} %get-tuple-element.44, pred[8,32,128]{2,1,0:T(8,128)(4,1)S(1)} %compare_and_fusion, bf16[8,32,128,128]{3,2,1,0:T(8,128)(2,1)} %bitcast.62), kind=kLoop, calls=%fused_computation.16 | loop fusion | flops 29360128 | bytes 25199872 | tf_op jit(solution)/shard_map/convert_element_type | solution.py:14
  712.1 90.3 %while.10 = (s32[]{:T(128)}, f32[8,64,32]{1,0,2:T(8,128)S(1)}, s32[8,32]{1,0:T(8,128)S(1)}, bf16[8,64,32,128]{3,2,1,0:T(8,128)(2,1)}, bf16[8,32,128,128]{3,2,1,0...) while((s32[]{:T(128)}, f32[8,64,32]{1,0,2:T(8,128)S(1)}, s32[8,32]{1,0:T(8,128)S(1)}, ...), condition=%wide.region_3.4_spmd, body=%wide.region_0.3_spmd.sunk | while | flops 2164264960 | bytes 2164193 | solution.py:52
  712.3 10.7 %select_reduce_fusion.2 = f32[64,32,32]{1,2,0:T(8,128)S(1)} fusion(pred[32,128]{1,0:T(8,128)(4,1)S(1)} %iota_compare_fusion.2, bf16[8,32,128,128]{3,2,1,0:T(8,128)(2,1)} %get-tuple-element.96, s32[]{:T(128)} %get-tuple-element.84, bf16[8,64,32,128]{3,2,1,0:T(8,128)(2,1)} %get-tuple-element.95), kind=kOutput, calls=%fused_computation.6.clone.1 | convolution fusion | flops 2164195328 | bytes 1840128 | tf_op jit(solution)/shard_map/while/body/eval_jaxpr/rd,cd->rc/dot_general | solution.py:20
  722.9 0.3 reduce_sum.10
  723.3 0.1 dynamic_update_slice.5
  723.5 10.7 %select_reduce_fusion.2 = f32[64,32,32]{1,2,0:T(8,128)S(1)} fusion(pred[32,128]{1,0:T(8,128)(4,1)S(1)} %iota_compare_fusion.2, bf16[8,32,128,128]{3,2,1,0:T(8,128)(2,1)} %get-tuple-element.96, s32[]{:T(128)} %get-tuple-element.84, bf16[8,64,32,128]{3,2,1,0:T(8,128)(2,1)} %get-tuple-element.95), kind=kOutput, calls=%fused_computation.6.clone.1 | convolution fusion | flops 2164195328 | bytes 1840128 | tf_op jit(solution)/shard_map/while/body/eval_jaxpr/rd,cd->rc/dot_general | solution.py:20
  734.2 0.3 reduce_sum.10
  734.8 10.7 %select_reduce_fusion.2 = f32[64,32,32]{1,2,0:T(8,128)S(1)} fusion(pred[32,128]{1,0:T(8,128)(4,1)S(1)} %iota_compare_fusion.2, bf16[8,32,128,128]{3,2,1,0:T(8,128)(2,1)} %get-tuple-element.96, s32[]{:T(128)} %get-tuple-element.84, bf16[8,64,32,128]{3,2,1,0:T(8,128)(2,1)} %get-tuple-element.95), kind=kOutput, calls=%fused_computation.6.clone.1 | convolution fusion | flops 2164195328 | bytes 1840128 | tf_op jit(solution)/shard_map/while/body/eval_jaxpr/rd,cd->rc/dot_general | solution.py:20
  745.5 0.3 reduce_sum.10
  745.9 0.1 dynamic_update_slice.5
  746.1 10.7 %select_reduce_fusion.2 = f32[64,32,32]{1,2,0:T(8,128)S(1)} fusion(pred[32,128]{1,0:T(8,128)(4,1)S(1)} %iota_compare_fusion.2, bf16[8,32,128,128]{3,2,1,0:T(8,128)(2,1)} %get-tuple-element.96, s32[]{:T(128)} %get-tuple-element.84, bf16[8,64,32,128]{3,2,1,0:T(8,128)(2,1)} %get-tuple-element.95), kind=kOutput, calls=%fused_computation.6.clone.1 | convolution fusion | flops 2164195328 | bytes 1840128 | tf_op jit(solution)/shard_map/while/body/eval_jaxpr/rd,cd->rc/dot_general | solution.py:20
  756.8 0.3 reduce_sum.10
  757.4 10.7 %select_reduce_fusion.2 = f32[64,32,32]{1,2,0:T(8,128)S(1)} fusion(pred[32,128]{1,0:T(8,128)(4,1)S(1)} %iota_compare_fusion.2, bf16[8,32,128,128]{3,2,1,0:T(8,128)(2,1)} %get-tuple-element.96, s32[]{:T(128)} %get-tuple-element.84, bf16[8,64,32,128]{3,2,1,0:T(8,128)(2,1)} %get-tuple-element.95), kind=kOutput, calls=%fused_computation.6.clone.1 | convolution fusion | flops 2164195328 | bytes 1840128 | tf_op jit(solution)/shard_map/while/body/eval_jaxpr/rd,cd->rc/dot_general | solution.py:20
  768.1 0.3 reduce_sum.10
  768.7 10.7 %select_reduce_fusion.2 = f32[64,32,32]{1,2,0:T(8,128)S(1)} fusion(pred[32,128]{1,0:T(8,128)(4,1)S(1)} %iota_compare_fusion.2, bf16[8,32,128,128]{3,2,1,0:T(8,128)(2,1)} %get-tuple-element.96, s32[]{:T(128)} %get-tuple-element.84, bf16[8,64,32,128]{3,2,1,0:T(8,128)(2,1)} %get-tuple-element.95), kind=kOutput, calls=%fused_computation.6.clone.1 | convolution fusion | flops 2164195328 | bytes 1840128 | tf_op jit(solution)/shard_map/while/body/eval_jaxpr/rd,cd->rc/dot_general | solution.py:20
  779.4 0.3 reduce_sum.10
  780.0 10.7 %select_reduce_fusion.2 = f32[64,32,32]{1,2,0:T(8,128)S(1)} fusion(pred[32,128]{1,0:T(8,128)(4,1)S(1)} %iota_compare_fusion.2, bf16[8,32,128,128]{3,2,1,0:T(8,128)(2,1)} %get-tuple-element.96, s32[]{:T(128)} %get-tuple-element.84, bf16[8,64,32,128]{3,2,1,0:T(8,128)(2,1)} %get-tuple-element.95), kind=kOutput, calls=%fused_computation.6.clone.1 | convolution fusion | flops 2164195328 | bytes 1840128 | tf_op jit(solution)/shard_map/while/body/eval_jaxpr/rd,cd->rc/dot_general | solution.py:20
  790.7 0.3 reduce_sum.10
  791.3 10.7 %select_reduce_fusion.2 = f32[64,32,32]{1,2,0:T(8,128)S(1)} fusion(pred[32,128]{1,0:T(8,128)(4,1)S(1)} %iota_compare_fusion.2, bf16[8,32,128,128]{3,2,1,0:T(8,128)(2,1)} %get-tuple-element.96, s32[]{:T(128)} %get-tuple-element.84, bf16[8,64,32,128]{3,2,1,0:T(8,128)(2,1)} %get-tuple-element.95), kind=kOutput, calls=%fused_computation.6.clone.1 | convolution fusion | flops 2164195328 | bytes 1840128 | tf_op jit(solution)/shard_map/while/body/eval_jaxpr/rd,cd->rc/dot_general | solution.py:20
  802.0 0.3 reduce_sum.10
  802.4 0.1 dynamic_update_slice.5
  802.5 0.1 copy.37
  802.7 0.8 reshape.251
  803.4 7.9 all-to-all-start
  811.3 9.7 %all-to-all-done = f32[128,1,128]{2,1,0:T(1,128)S(1)} async-done(((f32[128,1,128]{2,1,0:T(1,128)}), f32[128,1,128]{2,1,0:T(1,128)S(1)}, u32[]{:S(2)}, u32[]{:S(2)}) %all-to-all-start) | async-done | bytes 65568 | tf_op jit(solution)/shard_map/all_to_all | solution.py:65
  821.1 0.5 broadcast.179
  821.6 0.8 reduce
  822.4 0.1 reshape.252
  822.5 54.7 %gather_fusion.5 = f32[8192]{0:T(1024)S(1)} fusion(f32[64,256]{0,1:T(8,128)S(1)} %bitcast.58, s32[8192]{0:T(1024)S(1)} %fusion.6), kind=kCustom, calls=%fused_computation.5 | custom fusion | bytes 131072 | tf_op jit(solution)/shard_map/jit(take_along_axis)/gather | solution.py:67
  877.2 0.6 bitcast_select_fusion.1
  (58 shorter events, 1.9 us)
Async XLA Ops:
  6.5 4.7 copy-start
  6.5 203.4 %all-gather.5.cloned.1.call-start = ((), (), s32[]{:S(2)}) async-start(), calls=%async_computation.2 | async-start | bytes 35651584 | tf_op jit(solution)/shard_map/all_gather | solution.py:10
  7.3 704.9 %all-gather.3.cloned.1.call-start = ((), (), s32[]{:S(2)}) async-start(), calls=%async_computation.1 | async-start | bytes 4718592 | tf_op jit(solution)/shard_map/all_gather | solution.py:47
  56.2 9.2 %copy-start.2 = (s32[256]{0:T(256)S(1)}, s32[256]{0:T(256)}, u32[]{:S(2)}) copy-start(s32[256]{0:T(256)} %param.15) | copy-start | bytes 3076
  712.1 99.2 %copy-start.3 = (s32[64,128]{1,0:T(8,128)S(1)}, s32[64,128]{1,0:T(8,128)}, u32[]{:S(2)}) copy-start(s32[64,128]{1,0:T(8,128)} %param.17) | copy-start | bytes 98308
  803.4 17.6 %all-to-all-start = ((f32[128,1,128]{2,1,0:T(1,128)}), f32[128,1,128]{2,1,0:T(1,128)S(1)}, u32[]{:S(2)}, u32[]{:S(2)}) async-start(f32[128,1,128]{2,1,0:T(1,128)} %reshape.251), calls=%async_computation | async-start | bytes 131072 | tf_op jit(solution)/shard_map/all_to_all | solution.py:65
  822.5 55.3 %copy-start.1 = (s32[256,128]{1,0:T(8,128)S(1)}, s32[256,128]{1,0:T(8,128)}, u32[]{:S(2)}) copy-start(s32[256,128]{1,0:T(8,128)} %param.13) | copy-start | bytes 393220
Sparse Core Ops, SparseCore 0:
  9.5 200.4 all-gather.4
  211.7 32.1 all-gather.2
where the time goes:
time: 895 us; the launch traced here: 885 us
  local copies, waits for them, and re-layouts  610 us (68%)
  waiting for transfers between devices  153 us (17%)
  matrix products  85.3 us (10%)
  other arithmetic  14.7 us (2%)
  between operations  14 us (2%)
    gather x1, local copies, waits for them, and re-layouts, decompress(): base = jnp.take(table, codes.reshape(-1), axis=0).astype(jnp.float32)  493 us
    all_gather x1, waiting for transfers between devices, decompress(): table = lax.all_gather(centroids, 'member', axis=0, tiled=True)  142 us
    dot_general x8, matrix products, maxsim(): jnp.einsum('rd,cd->rc', query_block.reshape(count * qtokens, width), embe...  85.3 us
    gather x1, local copies, waits for them, and re-layouts, body(): return jnp.take_along_axis(dense, cand, axis=1)  54.7 us
    unnamed x13, local copies, waits for them, and re-layouts  34 us
    gather x1, local copies, waits for them, and re-layouts, body(): jnp.take(doc_resid.reshape(held, block * width), chosen, axis=0)  21.2 us
  transfers between devices with their start and end apart: 3, of which 2 were waited for; matrix products, arithmetic and copies ran while one was open for 64% of the time, Pallas kernels for 0%

commit v1 on v0

v1 whole, which is shorter than its diff:
```python
import jax
import jax.numpy as jnp
from jax import lax
from jax.experimental import pallas as pl
from jax.experimental.pallas import tpu as pltpu
from jax.sharding import PartitionSpec as P

f32 = jnp.float32
bf16 = jnp.bfloat16
GROUPS = 8
HALF = 16
TOKENS = 128
QROWS = 2048
TILE = 256
TILES = QROWS // TILE


def score_kernel(place, docs, table, resid, query, odd, scale, length, out, pairs_a, pairs_b, wide, embedded):
    group = pl.program_id(0)

    def gather(pairs, first, part, parts):
        count = HALF * TOKENS // parts
        for spot in range(count * part, count * (part + 1)):
            doc, token = divmod(spot, TOKENS)
            pairs[2 * spot : 2 * spot + 2, :] = table[place[(first + doc) * TOKENS + token]]

    def embed(pairs, half):
        base = pl.multiple_of((group * 2 + half) * HALF, HALF)
        odd_t = odd[pl.ds(base, HALF), :].T
        scale_t = scale[pl.ds(base, HALF), :].T
        length_t = length[pl.ds(base, HALF), :].T
        token = lax.broadcasted_iota(jnp.int32, (TOKENS, TOKENS), 0)
        for doc in range(HALF):
            wide[...] = pairs[2 * TOKENS * doc : 2 * TOKENS * (doc + 1), :].astype(f32)
            even_rows = wide[pl.ds(0, TOKENS, stride=2), :]
            odd_rows = wide[pl.ds(1, TOKENS, stride=2), :]
            center = jnp.where(odd_t[:, doc : doc + 1] > 0, odd_rows, even_rows)
            value = center + scale_t[:, doc : doc + 1] * resid[docs[base + doc]].astype(f32)
            value = jnp.where(token < length_t[:, doc : doc + 1], value, value[0:1, :])
            embedded[TOKENS * doc : TOKENS * (doc + 1), :] = value.astype(bf16)

    def compute(half, feed):
        total = None
        for tile in range(TILES):
            feed(tile)
            sims = lax.dot_general(
                embedded[...],
                query[0, TILE * tile : TILE * (tile + 1), :],
                (((1,), (1,)), ((), ())),
                preferred_element_type=f32,
            )
            best = jnp.max(sims.reshape(HALF, TOKENS, TILE), axis=1)
            best = best[:, :128] + best[:, 128:]
            total = best if total is None else total + best
        total = (total + pltpu.roll(total, 64, 1)) * (1.0 / 32)
        lane = lax.broadcasted_iota(jnp.int32, (8, 128), 1)
        out[8 * half : 8 * half + 8, :] = jnp.where(lane < 64, total[:8], total[8:])

    @pl.when(group == 0)
    def _():
        gather(pairs_a, 0, 0, 1)

    embed(pairs_a, 0)
    compute(0, lambda tile: gather(pairs_b, (group * 2 + 1) * HALF, tile, TILES))
    embed(pairs_b, 1)
    following = jnp.minimum(group + 1, GROUPS - 1) * 2 * HALF
    compute(1, lambda tile: gather(pairs_a, following, tile, TILES))


def score(place, docs, table, resid, query, odd, scale, length):
    whole = pl.BlockSpec(memory_space=pltpu.VMEM)
    return pl.pallas_call(
        score_kernel,
        grid_spec=pltpu.PrefetchScalarGridSpec(
            num_scalar_prefetch=2,
            grid=(GROUPS,),
            in_specs=[
                whole,
                whole,
                pl.BlockSpec((1, QROWS, 128), lambda group, *_: (group, 0, 0)),
                whole,
                whole,
                whole,
            ],
            out_specs=pl.BlockSpec((16, 128), lambda group, *_: (group, 0)),
            scratch_shapes=[
                pltpu.VMEM((HALF * TOKENS * 2, 128), bf16),
                pltpu.VMEM((HALF * TOKENS * 2, 128), bf16),
                pltpu.VMEM((TOKENS * 2, 128), f32),
                pltpu.VMEM((HALF * TOKENS, 128), bf16),
            ],
        ),
        out_shape=jax.ShapeDtypeStruct((128, 128), f32),
        compiler_params=pltpu.CompilerParams(vmem_limit_bytes=60 << 20),
        name="score",
    )(place, docs, table, resid, query, odd, scale, length)


def pick_kernel(held, cand, out):
    turned = held[...].T
    source = cand[...] // 2
    first = jnp.take_along_axis(turned[:64], source, axis=1, mode="promise_in_bounds")
    second = jnp.take_along_axis(turned[64:], source, axis=1, mode="promise_in_bounds")
    out[...] = jnp.where(cand[...] % 2 == 0, first, second)


def pick(held, cand):
    return pl.pallas_call(
        pick_kernel, out_shape=jax.ShapeDtypeStruct((64, 128), f32), name="pick"
    )(held, cand)


def body(queries, centroids, doc_resid, doc_codes, doc_scale, doc_len, send_list, cand):
    axes = ("group", "member")
    group = lax.axis_index("group")
    part = lax.dynamic_slice_in_dim(centroids, group * 1024, 1024, 0)
    table = lax.all_gather(part.reshape(512, 2, 128), axes, axis=0, tiled=True)
    turned = queries.transpose(1, 0, 2).reshape(QROWS, 128)
    query = lax.all_gather(turned, "group", axis=0)
    docs = send_list[0].reshape(8, 2, 8, 2).transpose(0, 1, 3, 2).reshape(-1)
    codes = jnp.take(doc_codes, docs, axis=0, mode="clip")
    row = (((codes >> 10) & 7) * 16 + (codes >> 13)) * 1024 + (codes & 1023)
    scale = jnp.take(doc_scale, docs, axis=0, mode="clip").astype(f32)
    length = jnp.take(doc_len, docs, axis=0, mode="clip")
    spread = lambda x: jnp.broadcast_to(x[:, None], (256, 128))
    scores = score(
        (row >> 1).reshape(-1), docs, table, doc_resid, query, row & 1, spread(scale), spread(length)
    )
    held = lax.all_to_all(scores, axes, split_axis=0, concat_axis=0, tiled=True)
    return pick(held, cand)


def solution(mesh):
    placed = (
        P("group", None, None),
        P("member", None),
        P(("group", "member"), None, None),
        P(("group", "member"), None),
        P(("group", "member")),
        P(("group", "member")),
        P(("group", "member"), None, None),
        P("group", "member"),
    )
    return jax.shard_map(
        body, mesh=mesh, in_specs=placed, out_specs=P("group", "member"), check_vma=False
    )
```

time: 895 us -> 265 us (0.30); the launches traced: 885 us -> 265 us
  local copies, waits for them, and re-layouts: 610 us -> 10.8 us
  matrix products: 85.3 us -> 0 us
  Pallas kernels: 0 us -> 84.6 us
  blocking collectives: 0 us -> 17.4 us
  waiting for transfers between devices: 153 us -> 138 us
  other arithmetic: 14.7 us -> 0.76 us
    gather x8 -> x3, local copies, waits for them, and re-layouts: 573 us -> 5.48 us  [the longest x1 1.95 us: body(): length = jnp.take(doc_len, docs, axis=0, mode='clip')]
    dot_general x8 -> x0, matrix products: 85.3 us -> none  [maxsim(): jnp.einsum('rd,cd->rc', query_block.reshape(count * qtokens, width), embe...]
    pallas_call x0 -> x2, Pallas kernels: none -> 84.6 us  [the longest x1 83 us: score(): pl.pallas_call(score_kernel, grid_spec=pltpu.PrefetchScalarGridSpec(num_s...]
    unnamed x13 -> x6, local copies, waits for them, and re-layouts: 34 us -> 0.01 us
    all_to_all x0 -> x1, blocking collectives: none -> 17.4 us  [body(): held = lax.all_to_all(scores, axes, split_axis=0, concat_axis=0, tiled=True)]
    all_to_all x1 -> x0, waiting for transfers between devices: 9.73 us -> none  [body(): lax.all_to_all(local, ('group', 'member'), split_axis=0, concat_axis=0, t...]
    convert_element_type x2 -> x0, other arithmetic: 9.51 us -> none  [the longest x1 9.51 us: decompress(): return (base + spread).astype(jnp.bfloat16)]
  transfers between devices with their start and end apart: 3 -> 2, of which waited for: 2 -> 2; matrix products, arithmetic and copies ran while one was open for 64% -> 3% of each run, Pallas kernels for 0% -> 0%
where the time goes in v1:
time: 265 us
  waiting for transfers between devices  138 us (52%)
  Pallas kernels  84.6 us (32%)
  blocking collectives  17.4 us (7%)
  between operations  13.5 us (5%)
  local copies, waits for them, and re-layouts  10.8 us (4%)
    all_gather x1, waiting for transfers between devices, body(): table = lax.all_gather(part.reshape(512, 2, 128), axes, axis=0, tiled=True)  110 us
    pallas_call x1, Pallas kernels, score(): pl.pallas_call(score_kernel, grid_spec=pltpu.PrefetchScalarGridSpec(num_s...  83 us
    all_gather x1, waiting for transfers between devices, body(): query = lax.all_gather(turned, 'group', axis=0)  28.1 us
    all_to_all x1, blocking collectives, body(): held = lax.all_to_all(scores, axes, split_axis=0, concat_axis=0, tiled=True)  17.4 us
  transfers between devices with their start and end apart: 2, of which 2 were waited for; matrix products, arithmetic and copies ran while one was open for 3% of the time, Pallas kernels for 0%

profile of v1, /device:TPU:1, one launch (start us, length us, event | category | flops | bytes accessed | tf_op | source)
XLA Modules:
  0.0 265.0 jit_solution(10731192805724909462)
XLA Ops:
  6.5 0.0 copy-start
  6.5 0.0 copy-start.1
  6.5 0.0 all-gather.5.cloned.1.call-start
  6.5 2.2 copy.13
  8.8 0.0 all-gather.5.cloned.1.call-update
  8.8 0.0 all-gather.3.cloned.1.call-start
  8.8 0.0 copy-done
  8.8 0.7 constant_dynamic-slice_fusion
  9.6 0.0 all-gather.3.cloned.1.call-update
  9.6 0.8 reshape_squeeze.3
  10.4 0.1 reshape.35.docs
  10.5 0.0 copy-start.2
  10.5 1.6 gather_fusion
  12.1 1.9 gather_fusion.1
  14.0 0.0 copy-done.1
  14.1 1.9 gather_fusion.2
  16.0 0.8 fusion
  16.8 28.1 %all-gather.5.cloned.1.call-done.query = bf16[8,2048,128]{2,1,0:T(8,128)(2,1)} async-done(((bf16[1,2048,128]{2,1,0:T(8,128)(2,1)}), bf16[8,2048,128]{2,1,0:T(8,128)(2,1)}) %all-gather.5.cloned.1.call-update) | async-done | bytes 4194320 | tf_op jit(solution)/shard_map/all_gather | solution.py:119
  44.9 109.9 %all-gather.3.cloned.1.call-done.table = bf16[65536,2,128]{2,1,0:T(2,128)(2,1)} async-done(((bf16[512,2,128]{2,1,0:T(2,128)(2,1)}), bf16[65536,2,128]{2,1,0:T(2,128)(2,1)}) %all-gather.3.cloned.1.call-update) | async-done | bytes 33554448 | tf_op jit(solution)/shard_map/all_gather | solution.py:117
  154.7 0.8 broadcast_in_dim.13.scale
  155.5 0.7 broadcast_in_dim.22.length
  156.2 0.0 copy-done.2
  156.2 83.0 %score.1 = f32[128,128]{1,0:T(8,128)} custom-call(s32[32768]{0:T(1024)} %get-tuple-element.6.place, s32[256]{0:T(256)} %copy-done.2, bf16[65536,2,128]{2,1,0:T(2,128)(2,1)} %all-gather.3.cloned.1.call-done.table, bf16[256,128,128]{2,1,0:T(8,128)(2,1)} %resid.1, bf16[8,2048,128]{2,1,0:T(8,128)(2,1)} %all-gather.5.cloned.1.call-done.query, ...), custom_call_target="tpu_custom_call" | custom-call | tf_op jit(solution)/shard_map/score/pallas_call | solution.py:72
  239.2 17.4 %all_to_all.11 = f32[128,1,128]{2,1,0:T(1,128)} all-to-all(f32[128,1,128]{2,1,0:T(1,128)} %bitcast.17), channel_id=1, replica_groups=mesh['group'=8,'member'=16] {'group','member'}, dimensions={0} | all-to-all | bytes 131072 | tf_op jit(solution)/shard_map/all_to_all | solution.py:129
  256.5 1.7 pick.1
  (2 shorter events, 0.0 us)
Async XLA Ops:
  6.5 2.3 copy-start
  6.5 7.5 %copy-start.1 = (s32[256]{0:T(256)S(1)}, s32[256]{0:T(256)}, u32[]{:S(2)}) copy-start(s32[256]{0:T(256)} %param.13) | copy-start | bytes 3076
  6.5 38.3 %all-gather.5.cloned.1.call-start = ((), (), s32[]{:S(2)}) async-start(), calls=%async_computation.2 | async-start | bytes 4718592 | tf_op jit(solution)/shard_map/all_gather | solution.py:119
  8.8 145.9 %all-gather.3.cloned.1.call-start = ((), (), s32[]{:S(2)}) async-start(), calls=%async_computation.1 | async-start | bytes 33816576 | tf_op jit(solution)/shard_map/all_gather | solution.py:117
  10.5 145.7 %copy-start.2 = (s32[256]{0:T(256)}, s32[256]{0:T(256)S(1)}, u32[]{:S(2)}) copy-start(s32[256]{0:T(256)S(1)} %reshape.35.docs) | copy-start | bytes 3076
Sparse Core Ops, SparseCore 0:
  9.1 35.7 all-gather.4
  48.0 106.6 all-gather.2

commit v2 on v1

--- a/solution.py
+++ b/solution.py
@@ -15,7 +15,7 @@
 TILES = QROWS // TILE
 
 
-def score_kernel(place, docs, table, resid, query, odd, scale, length, out, pairs_a, pairs_b, wide, embedded):
+def score_kernel(own, place, docs, table, resid, query, odd, scale, length, out, pairs_a, pairs_b, wide, embedded):
     group = pl.program_id(0)
 
     def gather(pairs, first, part, parts):
@@ -67,17 +67,17 @@
     compute(1, lambda tile: gather(pairs_a, following, tile, TILES))
 
 
-def score(place, docs, table, resid, query, odd, scale, length):
+def score(own, place, docs, table, resid, query, odd, scale, length):
     whole = pl.BlockSpec(memory_space=pltpu.VMEM)
     return pl.pallas_call(
         score_kernel,
         grid_spec=pltpu.PrefetchScalarGridSpec(
-            num_scalar_prefetch=2,
+            num_scalar_prefetch=3,
             grid=(GROUPS,),
             in_specs=[
                 whole,
                 whole,
-                pl.BlockSpec((1, QROWS, 128), lambda group, *_: (group, 0, 0)),
+                pl.BlockSpec((1, QROWS, 128), lambda group, own, *_: (group ^ own[0], 0, 0)),
                 whole,
                 whole,
                 whole,
@@ -93,7 +93,7 @@
         out_shape=jax.ShapeDtypeStruct((128, 128), f32),
         compiler_params=pltpu.CompilerParams(vmem_limit_bytes=60 << 20),
         name="score",
-    )(place, docs, table, resid, query, odd, scale, length)
+    )(own, place, docs, table, resid, query, odd, scale, length)
 
 
 def pick_kernel(held, cand, out):
@@ -116,7 +116,10 @@
     part = lax.dynamic_slice_in_dim(centroids, group * 1024, 1024, 0)
     table = lax.all_gather(part.reshape(512, 2, 128), axes, axis=0, tiled=True)
     turned = queries.transpose(1, 0, 2).reshape(QROWS, 128)
-    query = lax.all_gather(turned, "group", axis=0)
+    query = turned[None]
+    for step in (1, 2, 4):
+        swapped = lax.ppermute(query, "group", [(g, g ^ step) for g in range(GROUPS)])
+        query = jnp.concatenate([query, swapped], axis=0)
     docs = send_list[0].reshape(8, 2, 8, 2).transpose(0, 1, 3, 2).reshape(-1)
     codes = jnp.take(doc_codes, docs, axis=0, mode="clip")
     row = (((codes >> 10) & 7) * 16 + (codes >> 13)) * 1024 + (codes & 1023)
@@ -124,6 +127,7 @@
     length = jnp.take(doc_len, docs, axis=0, mode="clip")
     spread = lambda x: jnp.broadcast_to(x[:, None], (256, 128))
     scores = score(
+        group[None].astype(jnp.int32),
         (row >> 1).reshape(-1), docs, table, doc_resid, query, row & 1, spread(scale), spread(length)
     )
     held = lax.all_to_all(scores, axes, split_axis=0, concat_axis=0, tiled=True)

time: 265 us -> 271 us (1.023)
  waiting for transfers between devices: 138 us -> 132 us
  starting transfers between devices: 0.04 us -> 5.96 us
  other arithmetic: 0.76 us -> 6.01 us
    ppermute x0 -> x3, waiting for transfers between devices: none -> 77.9 us  [body(): lax.ppermute(query, 'group', [(g, g ^ step) for g in range(GROUPS)])]
    all_gather x1, waiting for transfers between devices: 110 us -> 54.1 us  [body(): table = lax.all_gather(part.reshape(512, 2, 128), axes, axis=0, tiled=True)]
    all_gather x1 -> x0, waiting for transfers between devices: 28.1 us -> none  [body(): query = lax.all_gather(turned, 'group', axis=0)]
    ppermute x0 -> x3, starting transfers between devices: none -> 5.96 us  [body(): lax.ppermute(query, 'group', [(g, g ^ step) for g in range(GROUPS)])]
    concatenate x0 -> x3, other arithmetic: none -> 5.26 us  [body(): query = jnp.concatenate([query, swapped], axis=0)]
  transfers between devices with their start and end apart: 2 -> 4, of which waited for: 2 -> 4; matrix products, arithmetic and copies ran while one was open for 3% -> 4% of each run, Pallas kernels for 0% -> 0%
where the time goes in v2:
time: 271 us; the launch traced here: 270 us
  waiting for transfers between devices  132 us (49%)
  Pallas kernels  84.8 us (31%)
  blocking collectives  17.3 us (6%)
  between operations  13.5 us (5%)
  local copies, waits for them, and re-layouts  10.8 us (4%)
  other arithmetic  6.01 us (2%)
  starting transfers between devices  5.96 us (2%)
    pallas_call x1, Pallas kernels, score(): pl.pallas_call(score_kernel, grid_spec=pltpu.PrefetchScalarGridSpec(num_s...  83.1 us
    ppermute x3, waiting for transfers between devices, body(): lax.ppermute(query, 'group', [(g, g ^ step) for g in range(GROUPS)])  77.9 us
    all_gather x1, waiting for transfers between devices, body(): table = lax.all_gather(part.reshape(512, 2, 128), axes, axis=0, tiled=True)  54.1 us
    all_to_all x1, blocking collectives, body(): held = lax.all_to_all(scores, axes, split_axis=0, concat_axis=0, tiled=True)  17.3 us
    ppermute x3, starting transfers between devices, body(): lax.ppermute(query, 'group', [(g, g ^ step) for g in range(GROUPS)])  5.96 us
  transfers between devices with their start and end apart: 4, of which 4 were waited for; matrix products, arithmetic and copies ran while one was open for 4% of the time, Pallas kernels for 0%

profile of v2, /device:TPU:1, one launch (start us, length us, event | category | flops | bytes accessed | tf_op | source)
XLA Modules:
  0.0 270.3 jit_solution(17597701889086581842)
XLA Ops:
  6.5 0.0 copy-start
  6.5 0.0 copy-start.6
  6.5 0.0 copy-start.3
  6.5 0.0 all-gather.2.cloned.1.call-start
  6.6 1.6 copy-done
  8.1 0.7 constant_dynamic-slice_fusion
  8.8 0.0 all-gather.2.cloned.1.call-update
  8.9 0.0 copy-start.1
  8.9 1.3 copy.13
  10.1 0.0 copy-start.2
  10.1 1.5 collective-permute-start
  11.6 1.5 collective-permute-done
  13.2 0.1 pad_maximum_fusion.2
  13.3 1.5 collective-permute-start.1
  14.7 25.8 %collective-permute-done.1 = bf16[2,2048,128]{2,1,0:T(8,128)(2,1)S(1)} collective-permute-done((bf16[2,2048,128]{2,1,0:T(8,128)(2,1)S(1)}, bf16[2,2048,128]{2,1,0:T(8,128)(2,1)S(1)}, u32[]{:S(2)}, u32[]{:S(2)}) %collective-permute-start.1) | collective-permute-done | bytes 1048608 | tf_op jit(solution)/shard_map/ppermute | solution.py:121
  40.5 0.0 copy-start.4
  40.5 1.0 copy-done.4
  41.5 1.5 pad_maximum_fusion.1
  43.1 3.0 %collective-permute-start.2 = (bf16[4,2048,128]{2,1,0:T(8,128)(2,1)}, bf16[4,2048,128]{2,1,0:T(8,128)(2,1)}, u32[]{:S(2)}, u32[]{:S(2)}) collective-permute-start(bf16[4,2048,128]{2,1,0:T(8,128)(2,1)} %pad_maximum_fusion.1), channel_id=1, source_target_pairs={{0,64},{16,80},{32,96},{48,112},{64,0},{80,16},{96,32},{112,48},{1... | collective-permute-start | bytes 6291464 | tf_op jit(solution)/shard_map/ppermute | solution.py:121
  46.1 0.0 copy-done.6
  46.1 0.1 reshape_squeeze.3
  46.2 0.1 reshape.35.docs
  46.3 0.0 copy-start.5
  46.3 0.0 copy-done.3
  46.3 0.7 gather_fusion
  47.0 0.0 copy-done.1
  47.0 1.9 gather_fusion.2
  49.0 0.0 copy-done.2
  49.0 1.9 gather_fusion.1
  50.9 0.7 fusion
  51.6 50.5 %collective-permute-done.2 = bf16[4,2048,128]{2,1,0:T(8,128)(2,1)} collective-permute-done((bf16[4,2048,128]{2,1,0:T(8,128)(2,1)}, bf16[4,2048,128]{2,1,0:T(8,128)(2,1)}, u32[]{:S(2)}, u32[]{:S(2)}) %collective-permute-start.2) | collective-permute-done | bytes 2097184 | tf_op jit(solution)/shard_map/ppermute | solution.py:121
  102.2 3.6 %pad_maximum_fusion.query = bf16[8,2048,128]{2,1,0:T(8,128)(2,1)} fusion(bf16[4,2048,128]{2,1,0:T(8,128)(2,1)} %collective-permute-done.2, bf16[2,2048,128]{2,1,0:T(8,128)(2,1)} %copy-done.4, bf16[1,2048,128]{2,1,0:T(8,128)(2,1)S(1)} %collective-permute-done, bf16[1,2048,128]{2,1,0:T(8,128)(2,1)S(1)} %bitcast.18), kind=kLoop, calls=%fused_computation.3 | loop fusion | flops 6291456 | bytes 8388608 | tf_op jit(solution)/shard_map/concatenate | solution.py:122
  105.8 0.0 copy-done.5
  105.8 54.1 %all-gather.2.cloned.1.call-done.table = bf16[65536,2,128]{2,1,0:T(2,128)(2,1)} async-done(((bf16[512,2,128]{2,1,0:T(2,128)(2,1)}), bf16[65536,2,128]{2,1,0:T(2,128)(2,1)}) %all-gather.2.cloned.1.call-update) | async-done | bytes 33554448 | tf_op jit(solution)/shard_map/all_gather | solution.py:117
  159.9 0.8 broadcast_in_dim.26.length
  160.7 0.7 broadcast_in_dim.25.scale
  161.4 83.1 %score.1 = f32[128,128]{1,0:T(8,128)} custom-call(s32[1]{0:T(128)} %bitcast.own, s32[32768]{0:T(1024)} %get-tuple-element.6.place, s32[256]{0:T(256)} %copy-done.5, bf16[65536,2,128]{2,1,0:T(2,128)(2,1)} %all-gather.2.cloned.1.call-done.table, bf16[256,128,128]{2,1,0:T(8,128)(2,1)} %resid.1, bf16[8,2048,128]{2,1,0:T(8,128)(2,1)} %pad_maximum_fusion.query, ...), custom_call_target="tpu_custom_call" | custom-call | tf_op jit(solution)/shard_map/score/pallas_call | solution.py:72
  244.5 17.3 %all_to_all.11 = f32[128,1,128]{2,1,0:T(1,128)} all-to-all(f32[128,1,128]{2,1,0:T(1,128)} %bitcast.21), channel_id=1, replica_groups=mesh['group'=8,'member'=16] {'group','member'}, dimensions={0} | all-to-all | bytes 131072 | tf_op jit(solution)/shard_map/all_to_all | solution.py:133
  261.8 1.7 pick.1
  (2 shorter events, 0.0 us)
Async XLA Ops:
  6.5 1.6 copy-start
  6.5 39.5 %copy-start.6 = (s32[1,128,2]{1,2,0:T(2,128)S(1)}, s32[1,128,2]{1,2,0:T(2,128)}, u32[]{:S(2)}) copy-start(s32[1,128,2]{1,2,0:T(2,128)} %param.14) | copy-start | bytes 3076
  6.5 39.8 %copy-start.3 = (s32[256,128]{1,0:T(8,128)S(1)}, s32[256,128]{1,0:T(8,128)}, u32[]{:S(2)}) copy-start(s32[256,128]{1,0:T(8,128)} %param.11) | copy-start | bytes 393220
  6.5 153.4 %all-gather.2.cloned.1.call-start = ((), (), s32[]{:S(2)}) async-start(), calls=%async_computation.1 | async-start | bytes 33816576 | tf_op jit(solution)/shard_map/all_gather | solution.py:117
  8.9 38.2 %copy-start.1 = (s32[256]{0:T(256)S(1)}, s32[256]{0:T(256)}, u32[]{:S(2)}) copy-start(s32[256]{0:T(256)} %param.13) | copy-start | bytes 3076
  10.1 38.9 %copy-start.2 = (bf16[256]{0:T(256)(128)(2,1)S(1)}, bf16[256]{0:T(256)(128)(2,1)}, u32[]{:S(2)}) copy-start(bf16[256]{0:T(256)(128)(2,1)} %param.12) | copy-start | bytes 1540
  10.1 3.0 %collective-permute-start = (bf16[1,2048,128]{2,1,0:T(8,128)(2,1)S(1)}, bf16[1,2048,128]{2,1,0:T(8,128)(2,1)S(1)}, u32[]{:S(2)}, u32[]{:S(2)}) collective-permute-start(bf16[1,2048,128]{2,1,0:T(8,128)(2,1)S(1)} %bitcast.15), channel_id=1, source_target_pairs={{0,16},{16,0},{32,48},{48,32},{64,80},{80,64},{96,112},{112,96},{1... | collective-permute-start | bytes 1572872 | tf_op jit(solution)/shard_map/ppermute | solution.py:121
  13.3 27.3 %collective-permute-start.1 = (bf16[2,2048,128]{2,1,0:T(8,128)(2,1)S(1)}, bf16[2,2048,128]{2,1,0:T(8,128)(2,1)S(1)}, u32[]{:S(2)}, u32[]{:S(2)}) collective-permute-start(bf16[2,2048,128]{2,1,0:T(8,128)(2,1)S(1)} %pad_maximum_fusion.2), channel_id=1, source_target_pairs={{0,32},{16,48},{32,0},{48,16},{64,96},{80,112},{96,64},{112,80},{1... | collective-permute-start | bytes 3145736 | tf_op jit(solution)/shard_map/ppermute | solution.py:121
  40.5 1.0 copy-start.4
  43.1 59.1 %collective-permute-start.2 = (bf16[4,2048,128]{2,1,0:T(8,128)(2,1)}, bf16[4,2048,128]{2,1,0:T(8,128)(2,1)}, u32[]{:S(2)}, u32[]{:S(2)}) collective-permute-start(bf16[4,2048,128]{2,1,0:T(8,128)(2,1)} %pad_maximum_fusion.1), channel_id=1, source_target_pairs={{0,64},{16,80},{32,96},{48,112},{64,0},{80,16},{96,32},{112,48},{1... | collective-permute-start | bytes 6291464 | tf_op jit(solution)/shard_map/ppermute | solution.py:121
  46.3 59.5 %copy-start.5 = (s32[256]{0:T(256)}, s32[256]{0:T(256)S(1)}, u32[]{:S(2)}) copy-start(s32[256]{0:T(256)S(1)} %reshape.35.docs) | copy-start | bytes 3076
Sparse Core Ops, SparseCore 0:
  10.5 149.3 all-gather.1

commit v3 on v1

--- a/solution.py
+++ b/solution.py
@@ -12,6 +12,7 @@
 TOKENS = 128
 QROWS = 2048
 TILE = 256
+SENT = 1152
 TILES = QROWS // TILE
 
 
@@ -45,7 +46,7 @@
             feed(tile)
             sims = lax.dot_general(
                 embedded[...],
-                query[0, TILE * tile : TILE * (tile + 1), :],
+                query[0, 2 * tile : 2 * tile + 2].reshape(TILE, 128),
                 (((1,), (1,)), ((), ())),
                 preferred_element_type=f32,
             )
@@ -77,7 +78,7 @@
             in_specs=[
                 whole,
                 whole,
-                pl.BlockSpec((1, QROWS, 128), lambda group, *_: (group, 0, 0)),
+                pl.BlockSpec((1, 16, 128, 128), lambda group, *_: (group, 0, 8, 0)),
                 whole,
                 whole,
                 whole,
@@ -114,12 +115,15 @@
     axes = ("group", "member")
     group = lax.axis_index("group")
     part = lax.dynamic_slice_in_dim(centroids, group * 1024, 1024, 0)
-    table = lax.all_gather(part.reshape(512, 2, 128), axes, axis=0, tiled=True)
     turned = queries.transpose(1, 0, 2).reshape(QROWS, 128)
-    query = lax.all_gather(turned, "group", axis=0)
+    own = lax.dynamic_slice_in_dim(turned, lax.axis_index("member") * 128, 128, 0)
+    sent = jnp.concatenate([part, own], axis=0)
+    held = lax.all_gather(sent, axes, axis=0, tiled=True)
+    table = held.reshape(-1, 2, 128)
+    query = held.reshape(GROUPS, 16, SENT, 128)
     docs = send_list[0].reshape(8, 2, 8, 2).transpose(0, 1, 3, 2).reshape(-1)
     codes = jnp.take(doc_codes, docs, axis=0, mode="clip")
-    row = (((codes >> 10) & 7) * 16 + (codes >> 13)) * 1024 + (codes & 1023)
+    row = (((codes >> 10) & 7) * 16 + (codes >> 13)) * SENT + (codes & 1023)
     scale = jnp.take(doc_scale, docs, axis=0, mode="clip").astype(f32)
     length = jnp.take(doc_len, docs, axis=0, mode="clip")
     spread = lambda x: jnp.broadcast_to(x[:, None], (256, 128))

time: 265 us -> 239 us (0.902)
  waiting for transfers between devices: 138 us -> 111 us
    all_gather x2 -> x1, waiting for transfers between devices: 138 us -> 111 us  [body(): held = lax.all_gather(sent, axes, axis=0, tiled=True)]
  transfers between devices with their start and end apart: 2 -> 1, of which waited for: 2 -> 1; matrix products, arithmetic and copies ran while one was open for 3% -> 3% of each run, Pallas kernels for 0% -> 0%
where the time goes in v3:
time: 239 us
  waiting for transfers between devices  111 us (46%)
  Pallas kernels  85.9 us (36%)
  blocking collectives  17.5 us (7%)
  between operations  13.4 us (6%)
  local copies, waits for them, and re-layouts  9.64 us (4%)
    all_gather x1, waiting for transfers between devices, body(): held = lax.all_gather(sent, axes, axis=0, tiled=True)  111 us
    pallas_call x1, Pallas kernels, score(): pl.pallas_call(score_kernel, grid_spec=pltpu.PrefetchScalarGridSpec(num_s...  84.2 us
    all_to_all x1, blocking collectives, body(): held = lax.all_to_all(scores, axes, split_axis=0, concat_axis=0, tiled=True)  17.5 us
  transfers between devices with their start and end apart: 1, of which 1 were waited for; matrix products, arithmetic and copies ran while one was open for 3% of the time, Pallas kernels for 0%

profile of v3, /device:TPU:1, one launch (start us, length us, event | category | flops | bytes accessed | tf_op | source)
XLA Modules:
  0.0 238.6 jit_solution(15741059218649989877)
XLA Ops:
  6.5 0.0 copy-start
  6.5 0.0 all-gather.2.cloned.1.call-start
  6.5 1.4 copy.13
  8.0 0.3 copy-done
  8.3 0.7 pad_maximum_fusion
  9.0 0.0 all-gather.2.cloned.1.call-update
  9.1 0.8 reshape_squeeze.3
  9.9 0.1 reshape.43.docs
  10.0 0.0 copy-start.1
  10.0 1.6 gather_fusion
  11.6 2.0 gather_fusion.2
  13.6 1.9 gather_fusion.1
  15.5 0.7 fusion
  16.2 110.6 %all-gather.2.cloned.1.call-done = bf16[147456,128]{1,0:T(8,128)(2,1)} async-done(((bf16[1152,128]{1,0:T(8,128)(2,1)}), bf16[147456,128]{1,0:T(8,128)(2,1)}) %all-gather.2.cloned.1.call-update) | async-done | bytes 37748752 | tf_op jit(solution)/shard_map/all_gather | solution.py:121
  126.8 0.7 broadcast_in_dim.22.length
  127.6 0.7 broadcast_in_dim.13.scale
  128.3 0.0 copy-done.1
  128.3 84.2 %score.1 = f32[128,128]{1,0:T(8,128)} custom-call(s32[32768]{0:T(1024)} %get-tuple-element.6.place, s32[256]{0:T(256)} %copy-done.1, bf16[73728,2,128]{2,1,0:T(2,128)(2,1)} %bitcast.15, bf16[256,128,128]{2,1,0:T(8,128)(2,1)} %resid.1, bf16[8,16,1152,128]{3,2,1,0:T(8,128)(2,1)} %bitcast.16, s32[256,128]{1,0:T(8,128)} %get-tuple-element.5.odd, ...), custom_call_target="tpu_custom_call" | custom-call | tf_op jit(solution)/shard_map/score/pallas_call | solution.py:73
  212.5 17.5 %all_to_all.11 = f32[128,1,128]{2,1,0:T(1,128)} all-to-all(f32[128,1,128]{2,1,0:T(1,128)} %bitcast.19), channel_id=1, replica_groups=mesh['group'=8,'member'=16] {'group','member'}, dimensions={0} | all-to-all | bytes 131072 | tf_op jit(solution)/shard_map/all_to_all | solution.py:133
  230.1 1.7 pick.1
  (4 shorter events, 0.0 us)
Async XLA Ops:
  6.5 1.7 copy-start
  6.5 120.3 %all-gather.2.cloned.1.call-start = ((), (), s32[]{:S(2)}) async-start(), calls=%async_computation.1 | async-start | bytes 38043648 | tf_op jit(solution)/shard_map/all_gather | solution.py:121
  10.0 118.4 %copy-start.1 = (s32[256]{0:T(256)}, s32[256]{0:T(256)S(1)}, u32[]{:S(2)}) copy-start(s32[256]{0:T(256)S(1)} %reshape.43.docs) | copy-start | bytes 3076
Sparse Core Ops, SparseCore 0:
  10.2 116.5 all-gather.1
